TPU v7x, 32 devices: a whole 2x2x4 slice. The times are simulated.
32 devices in a mesh: dp: 8 (over y, x, core), tensor: 4 (over z).
Axes of the slice: x: 2, y: 2, z: 4, core: 2. Of those that a mesh axis runs over, the one named last changes fastest.
Arguments:
- tokens: bfloat16 [32768, 768], P(('dp', 'tensor')), may hold values from -6 to 6
- qkv_weight: bfloat16 [768, 3, 768], P('dp', None, 'tensor'), may hold values from -0.3125 to 0.3125
- qv_bias: float32 [2, 768], replicated, may hold values from -3 to 3
- out_weight: bfloat16 [768, 768], P('dp', 'tensor'), may hold values from -0.875 to 0.875
- out_bias: float32 [768], replicated, may hold values from -2 to 2
- norm1_gain: float32 [768], replicated, may hold values from 0.1 to 1.9
- norm1_shift: float32 [768], replicated, may hold values from -2 to 2
- in_weight: bfloat16 [768, 2, 3072], P('dp', None, 'tensor'), may hold values from -0.21875 to 0.21875
- down_weight: bfloat16 [768, 3072], P('dp', 'tensor'), may hold values from -0.15625 to 0.15625
- down_bias: float32 [768], replicated, may hold values from -2 to 2
- norm2_gain: float32 [768], replicated, may hold values from 0.1 to 1.9
- norm2_shift: float32 [768], replicated, may hold values from -2 to 2
- cotangent: bfloat16 [32768, 768], P(('dp', 'tensor')), may hold values from -6 to 6
Outputs:
- layer_out: bfloat16 [32768, 768], P(('dp', 'tensor'))
- tokens_grad: bfloat16 [32768, 768], P(('dp', 'tensor'))
- qkv_weight_grad: float32 [768, 3, 768], P('dp', None, 'tensor')
- qv_bias_grad: float32 [2, 768], replicated
- out_weight_grad: float32 [768, 768], P('dp', 'tensor')
- out_bias_grad: float32 [768], replicated
- norm1_gain_grad: float32 [768], replicated
- norm1_shift_grad: float32 [768], replicated
- in_weight_grad: float32 [768, 2, 3072], P('dp', None, 'tensor')
- down_weight_grad: float32 [768, 3072], P('dp', 'tensor')
- down_bias_grad: float32 [768], replicated
- norm2_gain_grad: float32 [768], replicated
- norm2_shift_grad: float32 [768], replicated
All inputs are finite; a program needn't handle non-finite values.
Results may differ from a plain program's by a relative error of at most 0.02.
The roundings to bfloat16 on the way count: a program that leaves them out, or rounds other values in their place, can miss the bound.
Values may be sent and summed in bfloat16 or wider, within the bound.
No kernel may reach another device: no remote copies, remote signals or barrier semaphores. Data moves between devices by JAX's collectives and lax.ppermute only.
A program may use at most 192 MiB of HBM per device.

v0:
```python
import math
import jax
import jax.numpy as jnp
from jax import lax
from jax.sharding import PartitionSpec as P

HEAD = 64
SEQ = 1024
NORM_EPS = 1e-12
INV_ROOT_TWO = 0.7071067811865476
INV_ROOT_TWO_PI = 0.3989422804014327


def head_slopes(first_head, head_count):
    head_ids = first_head + jnp.arange(head_count, dtype=jnp.int32)
    powers = jnp.where(
        head_ids < 8, -(head_ids + 1).astype(jnp.float32), 7.5 - head_ids.astype(jnp.float32)
    )
    return jnp.exp2(powers)


def norm_forward(resid, gain, shift):
    center = resid - jnp.mean(resid, axis=1, keepdims=True)
    inverse = lax.rsqrt(jnp.mean(center * center, axis=1, keepdims=True) + NORM_EPS)
    normed = center * inverse
    return (normed * gain + shift, normed, inverse)


def norm_backward(grad_rows, normed, inverse, gain):
    scaled = grad_rows * gain
    first_mean = jnp.mean(scaled, axis=1, keepdims=True)
    second_mean = jnp.mean(scaled * normed, axis=1, keepdims=True)
    d_resid = inverse * (scaled - first_mean - normed * second_mean)
    return (d_resid, jnp.sum(grad_rows * normed, axis=0), jnp.sum(grad_rows, axis=0))


def make_scores(queries, key_rows, slope_value):
    length = queries.shape[0]
    position = jnp.arange(length, dtype=jnp.float32)
    distance = jnp.abs(position[:, None] - position[None, :])
    raw_scores = jnp.einsum("qd,kd->qk", queries, key_rows, preferred_element_type=jnp.float32)
    return raw_scores * (1.0 / math.sqrt(queries.shape[1])) - slope_value * distance


def attend_forward(item):
    queries, key_rows, value_rows, slope_value = item
    scores = make_scores(queries, key_rows, slope_value)
    row_max = jnp.max(scores, axis=1, keepdims=True)
    weights = jnp.exp(scores - row_max)
    row_sum = jnp.sum(weights, axis=1, keepdims=True)
    probs_low = (weights / row_sum).astype(jnp.bfloat16)
    context = jnp.dot(probs_low, value_rows, preferred_element_type=jnp.float32).astype(
        jnp.bfloat16
    )
    return (context, (row_max + jnp.log(row_sum))[:, 0])


def attend_backward(item):
    queries, key_rows, value_rows, log_total, d_context, slope_value = item
    scores = make_scores(queries, key_rows, slope_value)
    probs = jnp.exp(scores - log_total[:, None])
    probs_low = probs.astype(jnp.bfloat16)
    d_values = jnp.einsum("qk,qd->kd", probs_low, d_context, preferred_element_type=jnp.float32)
    d_probs = jnp.einsum("qd,kd->qk", d_context, value_rows, preferred_element_type=jnp.float32)
    inner_sum = jnp.sum(probs * d_probs, axis=1, keepdims=True)
    d_scores = (probs * (d_probs - inner_sum)).astype(jnp.bfloat16)
    scale_factor = 1.0 / math.sqrt(queries.shape[1])
    d_queries = jnp.dot(d_scores, key_rows, preferred_element_type=jnp.float32) * scale_factor
    d_keys = (
        jnp.einsum("qk,qd->kd", d_scores, queries, preferred_element_type=jnp.float32)
        * scale_factor
    )
    return (d_queries, d_keys, d_values)


def to_items(matrix, head_count):
    seq_count = matrix.shape[0] // SEQ
    each_width = matrix.shape[1] // head_count
    shaped = matrix.reshape(seq_count, SEQ, head_count, each_width).transpose(0, 2, 1, 3)
    return shaped.reshape(seq_count * head_count, SEQ, each_width)


def from_items(items, head_count):
    seq_count = items.shape[0] // head_count
    shaped = items.reshape(seq_count, head_count, SEQ, items.shape[2]).transpose(0, 2, 1, 3)
    return shaped.reshape(seq_count * SEQ, head_count * items.shape[2])


def fetch_weights(qkv_weight, in_weight, out_weight, down_weight):
    qkv_rows, in_rows, out_rows, down_rows = (
        lax.all_gather(qkv_weight, "dp", axis=0, tiled=True),
        lax.all_gather(in_weight, "dp", axis=0, tiled=True),
        lax.all_gather(out_weight, "dp", axis=0, tiled=True),
        lax.all_gather(down_weight, "dp", axis=0, tiled=True),
    )
    return (qkv_rows, in_rows, out_rows, down_rows)


def gelu_parts(gate_part):
    normal_cdf = 0.5 * (1.0 + lax.erf(gate_part * INV_ROOT_TWO))
    density = jnp.exp(-0.5 * gate_part * gate_part) * INV_ROOT_TWO_PI
    return (gate_part * normal_cdf, normal_cdf + gate_part * density)


def local(
    tokens,
    qkv_weight,
    qv_bias,
    out_weight,
    out_bias,
    norm1_gain,
    norm1_shift,
    in_weight,
    down_weight,
    down_bias,
    norm2_gain,
    norm2_shift,
    cotangent,
):
    model_width = tokens.shape[1]
    qkv_full, in_full, out_full, down_full = fetch_weights(
        qkv_weight, in_weight, out_weight, down_weight
    )
    local_width = qkv_full.shape[2]
    hidden_width = in_full.shape[2]
    head_count = local_width // HEAD
    col_start = lax.axis_index("tensor") * local_width
    group_rows = lax.all_gather(tokens, "tensor", axis=0, tiled=True)
    seq_count = group_rows.shape[0] // SEQ
    item_slopes = jnp.tile(head_slopes(col_start // HEAD, head_count), seq_count)
    bias_local = lax.dynamic_slice_in_dim(qv_bias, col_start, local_width, 1)
    projected = jnp.dot(
        group_rows,
        qkv_full.reshape(model_width, 3 * local_width),
        preferred_element_type=jnp.float32,
    )
    queries = (projected[:, :local_width] + bias_local[0]).astype(jnp.bfloat16)
    key_rows = projected[:, local_width : 2 * local_width].astype(jnp.bfloat16)
    value_rows = (projected[:, 2 * local_width :] + bias_local[1]).astype(jnp.bfloat16)
    query_items = to_items(queries, head_count)
    key_items = to_items(key_rows, head_count)
    value_items = to_items(value_rows, head_count)
    context_items, log_totals = lax.map(
        attend_forward, (query_items, key_items, value_items, item_slopes)
    )
    context = from_items(context_items, head_count)
    attn_partial = jnp.einsum("rc,oc->ro", context, out_full, preferred_element_type=jnp.float32)
    attention = lax.psum_scatter(attn_partial, "tensor", scatter_dimension=0, tiled=True)
    resid1 = tokens.astype(jnp.float32) + attention + out_bias
    hidden1, normed1, inverse1 = norm_forward(resid1, norm1_gain, norm1_shift)
    hidden1_low = hidden1.astype(jnp.bfloat16)
    group_hidden = lax.all_gather(hidden1_low, "tensor", axis=0, tiled=True)
    gate_up = jnp.dot(
        group_hidden,
        in_full.reshape(model_width, 2 * hidden_width),
        preferred_element_type=jnp.float32,
    )
    gate_part = gate_up[:, :hidden_width]
    up_part = gate_up[:, hidden_width:]
    activated, slope_gelu = gelu_parts(gate_part)
    gated = (activated * up_part).astype(jnp.bfloat16)
    ffn_partial = jnp.einsum("rf,of->ro", gated, down_full, preferred_element_type=jnp.float32)
    ffn_out = lax.psum_scatter(ffn_partial, "tensor", scatter_dimension=0, tiled=True)
    resid2 = hidden1 + ffn_out + down_bias
    result, normed2, inverse2 = norm_forward(resid2, norm2_gain, norm2_shift)
    d_resid2, norm2_gain_grad, norm2_shift_grad = norm_backward(
        cotangent.astype(jnp.float32), normed2, inverse2, norm2_gain
    )
    down_bias_grad = jnp.sum(d_resid2, axis=0)
    d_ffn_low = d_resid2.astype(jnp.bfloat16)
    group_d_ffn = lax.all_gather(d_ffn_low, "tensor", axis=0, tiled=True)
    qkv_full, in_full, out_full, down_full = fetch_weights(
        qkv_weight, in_weight, out_weight, down_weight
    )
    d_gated = jnp.dot(group_d_ffn, down_full, preferred_element_type=jnp.float32)
    down_grad = jnp.einsum("ro,rf->of", group_d_ffn, gated, preferred_element_type=jnp.float32)
    d_gate_up = jnp.concatenate(
        [d_gated * up_part * slope_gelu, d_gated * activated], axis=1
    ).astype(jnp.bfloat16)
    in_grad = jnp.einsum(
        "rd,rc->dc", group_hidden, d_gate_up, preferred_element_type=jnp.float32
    ).reshape(model_width, 2, hidden_width)
    d_group_hidden = jnp.einsum(
        "rc,dc->rd",
        d_gate_up,
        in_full.reshape(model_width, 2 * hidden_width),
        preferred_element_type=jnp.float32,
    )
    d_hidden_ffn = lax.psum_scatter(d_group_hidden, "tensor", scatter_dimension=0, tiled=True)
    d_hidden1 = d_resid2 + d_hidden_ffn
    d_resid1, norm1_gain_grad, norm1_shift_grad = norm_backward(
        d_hidden1, normed1, inverse1, norm1_gain
    )
    out_bias_grad = jnp.sum(d_resid1, axis=0)
    d_attn_low = d_resid1.astype(jnp.bfloat16)
    group_d_attn = lax.all_gather(d_attn_low, "tensor", axis=0, tiled=True)
    d_context = jnp.dot(group_d_attn, out_full, preferred_element_type=jnp.float32).astype(
        jnp.bfloat16
    )
    out_grad = jnp.einsum("ro,rc->oc", group_d_attn, context, preferred_element_type=jnp.float32)
    d_query_items, d_key_items, d_value_items = lax.map(
        attend_backward,
        (
            query_items,
            key_items,
            value_items,
            log_totals,
            to_items(d_context, head_count),
            item_slopes,
        ),
    )
    d_queries = from_items(d_query_items, head_count)
    d_keys = from_items(d_key_items, head_count)
    d_values = from_items(d_value_items, head_count)
    bias_local_grad = jnp.stack([jnp.sum(d_queries, axis=0), jnp.sum(d_values, axis=0)])
    qv_grad = lax.dynamic_update_slice(
        jnp.zeros((2, model_width), jnp.float32),
        bias_local_grad,
        (jnp.zeros((), jnp.int32), col_start),
    )
    d_projected = jnp.concatenate([d_queries, d_keys, d_values], axis=1).astype(jnp.bfloat16)
    qkv_grad = jnp.einsum(
        "rd,rc->dc", group_rows, d_projected, preferred_element_type=jnp.float32
    ).reshape(model_width, 3, local_width)
    d_group_rows = jnp.einsum(
        "rc,dc->rd",
        d_projected,
        qkv_full.reshape(model_width, 3 * local_width),
        preferred_element_type=jnp.float32,
    )
    d_tokens_attn = lax.psum_scatter(
        d_group_rows.astype(jnp.bfloat16), "tensor", scatter_dimension=0, tiled=True
    ).astype(jnp.float32)
    tokens_grad = (d_resid1 + d_tokens_attn).astype(jnp.bfloat16)
    qkv_grad, in_grad, out_grad, down_grad = (
        lax.psum_scatter(qkv_grad, "dp", scatter_dimension=0, tiled=True),
        lax.psum_scatter(in_grad, "dp", scatter_dimension=0, tiled=True),
        lax.psum_scatter(out_grad, "dp", scatter_dimension=0, tiled=True),
        lax.psum_scatter(down_grad, "dp", scatter_dimension=0, tiled=True),
    )
    (
        qv_grad,
        out_bias_grad,
        norm1_gain_grad,
        norm1_shift_grad,
        down_bias_grad,
        norm2_gain_grad,
        norm2_shift_grad,
    ) = lax.psum(
        (
            qv_grad,
            out_bias_grad,
            norm1_gain_grad,
            norm1_shift_grad,
            down_bias_grad,
            norm2_gain_grad,
            norm2_shift_grad,
        ),
        ("dp", "tensor"),
    )
    return (
        result.astype(jnp.bfloat16),
        tokens_grad,
        qkv_grad,
        qv_grad,
        out_grad,
        out_bias_grad,
        norm1_gain_grad,
        norm1_shift_grad,
        in_grad,
        down_grad,
        down_bias_grad,
        norm2_gain_grad,
        norm2_shift_grad,
    )


def solution(mesh):
    placed = (
        P(("dp", "tensor"), None),
        P("dp", None, "tensor"),
        P(),
        P("dp", "tensor"),
        P(),
        P(),
        P(),
        P("dp", None, "tensor"),
        P("dp", "tensor"),
        P(),
        P(),
        P(),
        P(("dp", "tensor"), None),
    )
    return jax.shard_map(
        local,
        mesh=mesh,
        in_specs=placed,
        out_specs=(
            P(("dp", "tensor"), None),
            P(("dp", "tensor"), None),
            P("dp", None, "tensor"),
            P(),
            P("dp", "tensor"),
            P(),
            P(),
            P(),
            P("dp", None, "tensor"),
            P("dp", "tensor"),
            P(),
            P(),
            P(),
        ),
        check_vma=False,
    )
```

profile of v0, /device:TPU:0, one launch (start us, length us, event | category | flops | bytes accessed | tf_op | source)
XLA Modules:
  0.0 1840.1 jit_solution(1177063377857514128)
XLA Ops:
  10.0 14.6 all_gather.29
  25.5 8.5 all_gather.30
  34.9 93.6 %all-gather.7.cloned.1.call-done = bf16[4096,768]{1,0:T(8,128)(2,1)} async-done(((bf16[1024,768]{1,0:T(8,128)(2,1)}), bf16[4096,768]{1,0:T(8,128)(2,1)}) %all-gather.7.cloned.1.call-update) | async-done | bytes 6291472 | tf_op jit(solution)/shard_map/all_gather | solution.py:128
  160.1 131.6 %while.26 = (s32[]{:T(128)}, bf16[12,1024,64]{1,2,0:T(8,128)(2,1)}, f32[12,1024]{1,0:T(8,128)}, bf16[12,1024,64]{2,1,0:T(8,128)(2,1)S(1)}, bf16[12,1024,64]{2,1,...) while((s32[]{:T(128)}, bf16[12,1024,64]{1,2,0:T(8,128)(2,1)}, ...), condition=%wide.region_3.4_spmd, body=%wide.region_0.3_spmd.sunk | while | flops 280034304 | bytes 30321288 | solution.py:143
  304.5 209.3 %reduce-scatter.8.cloned.1.call-done = f32[1024,768]{1,0:T(8,128)} async-done(((f32[4096,768]{1,0:T(8,128)}), f32[1024,768]{1,0:T(8,128)}) %reduce-scatter.8.cloned.1.call-update) | async-done | bytes 3145744 | tf_op jit(solution)/shard_map/reduce_scatter | solution.py:148
  523.5 112.0 %all-gather.9.cloned.1.call-done = bf16[4096,768]{1,0:T(8,128)(2,1)} async-done(((bf16[1024,768]{1,0:T(8,128)(2,1)}), bf16[4096,768]{1,0:T(8,128)(2,1)}) %all-gather.9.cloned.1.call-update) | async-done | bytes 6291472 | tf_op jit(solution)/shard_map/all_gather | solution.py:152
  635.5 17.3 fusion.76
  652.8 12.2 multiply_convert_fusion.2
  665.0 10.4 fusion.77
  675.4 10.0 all-gather.15.cloned.1.call-start
  685.4 200.3 %reduce-scatter.10.cloned.1.call-done = f32[1024,768]{1,0:T(8,128)} async-done(((f32[4096,768]{1,0:T(8,128)}), f32[1024,768]{1,0:T(8,128)}) %reduce-scatter.10.cloned.1.call-update) | async-done | bytes 3145744 | tf_op jit(solution)/shard_map/reduce_scatter | solution.py:163
  898.2 116.5 %all-gather.15.cloned.1.call-done = bf16[4096,768]{1,0:T(8,128)(2,1)} async-done(((bf16[1024,768]{1,0:T(8,128)(2,1)}), bf16[4096,768]{1,0:T(8,128)(2,1)}) %all-gather.15.cloned.1.call-update) | async-done | bytes 6291472 | tf_op jit(solution)/shard_map/all_gather | solution.py:171
  1014.7 22.1 %fusion.50 = (bf16[4096,768]{0,1:T(8,128)(2,1)}, bf16[4096,768]{0,1:T(8,128)(2,1)}) fusion(f32[4096,1536]{0,1:T(8,128)} %fusion.76, bf16[4096,768]{1,0:T(8,128)(2,1)} %all-gather.15.cloned.1.call-done, bf16[768,768]{1,0:T(8,128)(2,1)} %all-gather.13.cloned.1.call-done), kind=kOutput, calls=%fused_computation.57 | convolution fusion | flops 4875878400 | bytes 45219840 | tf_op jit(solution)/shard_map/dot_general | solution.py:175
  1036.9 16.1 fusion.52
  1053.1 210.0 %reduce-scatter.12.cloned.1.call-done = f32[1024,768]{1,0:T(8,128)} async-done(((f32[4096,768]{1,0:T(8,128)}), f32[1024,768]{1,0:T(8,128)}) %reduce-scatter.12.cloned.1.call-update) | async-done | bytes 3145744 | tf_op jit(solution)/shard_map/reduce_scatter | solution.py:189
  1272.7 16.5 fusion.51
  1296.0 92.8 %all-gather.17.cloned.1.call-done = bf16[4096,768]{1,0:T(8,128)(2,1)} async-done(((bf16[1024,768]{1,0:T(8,128)(2,1)}), bf16[4096,768]{1,0:T(8,128)(2,1)}) %all-gather.17.cloned.1.call-update) | async-done | bytes 6291472 | tf_op jit(solution)/shard_map/all_gather | solution.py:196
  1403.3 167.5 %while.27 = (s32[]{:T(128)}, f32[12,1024,64]{1,2,0:T(8,128)S(1)}, bf16[12,1024,64]{1,2,0:T(8,128)(2,1)}, f32[12,1024,64]{1,2,0:T(8,128)}, bf16[12,1024,64]{2,1,0...) while((s32[]{:T(128)}, f32[12,1024,64]{1,2,0:T(8,128)S(1)}, ...), condition=%wide.region_17.18_spmd, body=%wide.region_15.17_spmd.sunk | while | flops 683801600 | bytes 34104956 | solution.py:201
  1589.5 10.5 fusion.80
  1627.3 47.4 %all-reduce.1 = (f32[2,768]{1,0:T(2,128)}, f32[768]{0:T(1024)}, f32[768]{0:T(1024)}, f32[768]{0:T(1024)}, f32[768]{0:T(1024)}, /*index=5*/f32[768]{0:T(1024)}, f32[768]{0:T(1024)}) all-reduce(f32[2,768]{1,0:T(2,128)S(1)} %dynamic_update_slice.21, f32[768]{0:T(1024)S(1)} %copy-done.23, ...), channel_id=1, replica_groups=mesh['dp'=8,'tensor'=4] {'dp','tensor'}, use_global_device_ids=true, to_apply=%region_22.23 | all-reduce | flops 6144 | bytes 49152 | tf_op jit(solution)/shard_map/psum | solution.py:249
  1674.8 24.9 %reduce-scatter.14.cloned.1.call-done = bf16[1024,768]{1,0:T(8,128)(2,1)} async-done(((bf16[4096,768]{1,0:T(8,128)(2,1)}), bf16[1024,768]{1,0:T(8,128)(2,1)}) %reduce-scatter.14.cloned.1.call-update) | async-done | bytes 1572880 | tf_op jit(solution)/shard_map/reduce_scatter | solution.py:231
  1702.5 44.0 %reduce-scatter.20.cloned.1.call-done = f32[96,768]{1,0:T(8,128)} async-done(((f32[768,768]{1,0:T(8,128)}), f32[96,768]{1,0:T(8,128)}) %reduce-scatter.20.cloned.1.call-update) | async-done | bytes 294928 | tf_op jit(solution)/shard_map/reduce_scatter | solution.py:239
  1746.5 39.0 %reduce-scatter.18.cloned.1.call-done = f32[96,192]{1,0:T(8,128)} async-done(((f32[768,192]{1,0:T(8,128)}), f32[96,192]{1,0:T(8,128)}) %reduce-scatter.18.cloned.1.call-update) | async-done | bytes 73744 | tf_op jit(solution)/shard_map/reduce_scatter | solution.py:238
  1785.5 46.8 %reduce-scatter.16.cloned.1.call-done = f32[96,3,192]{2,0,1:T(8,128)} async-done(((f32[768,3,192]{2,0,1:T(8,128)}), f32[96,3,192]{2,0,1:T(8,128)}) %reduce-scatter.16.cloned.1.call-update) | async-done | bytes 221200 | tf_op jit(solution)/shard_map/reduce_scatter | solution.py:236
  (353 shorter events, 447.3 us)
Async XLA Ops:
  8.0 17.5 copy-start.17
  8.0 120.5 %all-gather.7.cloned.1.call-start = ((), (), s32[]{:S(2)}) async-start(), calls=%async_computation.7 | async-start | bytes 7864320 | tf_op jit(solution)/shard_map/all_gather | solution.py:128
  8.8 505.1 %reduce-scatter.8.cloned.1.call-start = ((), (), s32[]{:S(2)}) async-start(), calls=%async_computation.8 | async-start | bytes 15728640 | tf_op jit(solution)/shard_map/reduce_scatter | solution.py:148
  25.5 109.0 %copy-start.13 = (bf16[768,3,192]{0,2,1:T(8,128)(2,1)}, bf16[768,3,192]{0,2,1:T(8,128)(2,1)S(1)}, u32[]{:S(2)}) copy-start(bf16[768,3,192]{0,2,1:T(8,128)(2,1)S(1)} %copy.42) | copy-start | bytes 2654212
  34.1 262.0 %copy-start.9 = (bf16[768,192]{1,0:T(8,128)(2,1)}, bf16[768,192]{1,0:T(8,128)(2,1)S(1)}, u32[]{:S(2)}) copy-start(bf16[768,192]{1,0:T(8,128)(2,1)S(1)} %all_gather.30) | copy-start | bytes 884740
  303.6 210.3 %copy-start.27 = (f32[768]{0:T(1024)S(1)}, f32[768]{0:T(1024)}, u32[]{:S(2)}) copy-start(f32[768]{0:T(1024)} %param.21) | copy-start | bytes 9220
  303.7 216.1 %all-gather.11.cloned.1.call-start = ((), (), s32[]{:S(2)}) async-start(), calls=%async_computation.10 | async-start | bytes 2654208 | tf_op jit(solution)/shard_map/all_gather | solution.py:92
  304.2 331.3 %all-gather.9.cloned.1.call-start = ((), (), s32[]{:S(2)}) async-start(), calls=%async_computation.9 | async-start | bytes 7864320 | tf_op jit(solution)/shard_map/all_gather | solution.py:152
  519.1 145.8 %all-gather.13.cloned.1.call-start = ((), (), s32[]{:S(2)}) async-start(), calls=%async_computation.11 | async-start | bytes 1327104 | tf_op jit(solution)/shard_map/all_gather | solution.py:94
  519.7 365.9 %reduce-scatter.10.cloned.1.call-start = ((), (), s32[]{:S(2)}) async-start(), calls=%async_computation.12 | async-start | bytes 15728640 | tf_op jit(solution)/shard_map/reduce_scatter | solution.py:163
  675.3 210.3 %copy-start.28 = (f32[768]{0:T(1024)S(1)}, f32[768]{0:T(1024)}, u32[]{:S(2)}) copy-start(f32[768]{0:T(1024)} %param.26) | copy-start | bytes 9220
  675.4 339.4 %all-gather.15.cloned.1.call-start = ((), (), s32[]{:S(2)}) async-start(), calls=%async_computation.13 | async-start | bytes 7864320 | tf_op jit(solution)/shard_map/all_gather | solution.py:171
  898.2 364.9 %reduce-scatter.12.cloned.1.call-start = ((), (), s32[]{:S(2)}) async-start(), calls=%async_computation.14 | async-start | bytes 15728640 | tf_op jit(solution)/shard_map/reduce_scatter | solution.py:189
  1014.7 22.1 %copy-start.11 = (bf16[96,8,2,768]{3,1,2,0:T(8,128)(2,1)S(1)}, bf16[96,8,2,768]{3,1,2,0:T(8,128)(2,1)}, u32[]{:S(2)}) copy-start(bf16[96,8,2,768]{3,1,2,0:T(8,128)(2,1)} %copy.53) | copy-start | bytes 7077892
  1053.0 335.8 %all-gather.17.cloned.1.call-start = ((), (), s32[]{:S(2)}) async-start(), calls=%async_computation.15 | async-start | bytes 7864320 | tf_op jit(solution)/shard_map/all_gather | solution.py:196
  1272.2 344.2 %all-reduce.4.cloned.1.call-start = ((), (), s32[]{:S(2)}) async-start(), calls=%async_computation.20 | async-start | bytes 9437184
  1295.9 92.9 %copy-start.10 = (bf16[768,192]{1,0:T(8,128)(2,1)S(1)}, bf16[768,192]{1,0:T(8,128)(2,1)}, u32[]{:S(2)}) copy-start(bf16[768,192]{1,0:T(8,128)(2,1)} %copy-done.9) | copy-start | bytes 884740
  1295.9 403.7 %reduce-scatter.14.cloned.1.call-start = ((), (), s32[]{:S(2)}) async-start(), calls=%async_computation.16 | async-start | bytes 7864320 | tf_op jit(solution)/shard_map/reduce_scatter | solution.py:231
  1589.5 10.6 copy-start.6
  1589.5 157.0 %reduce-scatter.20.cloned.1.call-start = ((), (), s32[]{:S(2)}) async-start(), calls=%async_computation.19 | async-start | bytes 2654208 | tf_op jit(solution)/shard_map/reduce_scatter | solution.py:239
  1600.0 185.5 %reduce-scatter.18.cloned.1.call-start = ((), (), s32[]{:S(2)}) async-start(), calls=%async_computation.18 | async-start | bytes 884736 | tf_op jit(solution)/shard_map/reduce_scatter | solution.py:238
  1605.6 226.7 %reduce-scatter.16.cloned.1.call-start = ((), (), s32[]{:S(2)}) async-start(), calls=%async_computation.17 | async-start | bytes 2654208 | tf_op jit(solution)/shard_map/reduce_scatter | solution.py:236
  1618.4 8.9 copy-start.24
  1618.5 81.2 %copy-start.3 = (f32[1024,768]{1,0:T(8,128)S(1)}, f32[1024,768]{1,0:T(8,128)}, u32[]{:S(2)}) copy-start(f32[1024,768]{1,0:T(8,128)} %copy-done.2) | copy-start | bytes 9437188
  (33 other events, 104.4 us)
Sparse Core Ops, SparseCore 0:
  10.4 118.0 all-gather.6
  303.8 210.0 reduce-scatter.7
  898.3 116.3 all-gather.14
  1272.4 116.3 all-gather.16
  1589.6 110.0 reduce-scatter.13
  1703.4 43.0 reduce-scatter.19
  1750.5 34.9 reduce-scatter.17
  1789.8 42.4 reduce-scatter.15
Sparse Core Ops, SparseCore 1:
  306.0 27.0 all-gather.10
  519.2 116.2 all-gather.8
  637.3 22.1 all-gather.12
  675.4 210.2 reduce-scatter.9
  1053.1 209.9 reduce-scatter.11
  1296.0 87.4 all-reduce.3
where the time goes:
time: 1850 us; the launch traced here: 1840 us
  waiting for transfers between devices  1190 us (64%)
  matrix products  346 us (19%)
  local copies, waits for them, and re-layouts  134 us (7%)
  blocking collectives  70.6 us (4%)
  other arithmetic  69.1 us (4%)
    reduce_scatter x1, waiting for transfers between devices, local(): lax.psum_scatter(d_group_hidden, 'tensor', scatter_dimension=0, tiled=True)  210 us
    reduce_scatter x1, waiting for transfers between devices, local(): lax.psum_scatter(attn_partial, 'tensor', scatter_dimension=0, tiled=True)  209 us
    reduce_scatter x1, waiting for transfers between devices, local(): lax.psum_scatter(ffn_partial, 'tensor', scatter_dimension=0, tiled=True)  200 us
    all_gather x1, waiting for transfers between devices, local(): group_d_ffn = lax.all_gather(d_ffn_low, 'tensor', axis=0, tiled=True)  116 us
    all_gather x1, waiting for transfers between devices, local(): group_hidden = lax.all_gather(hidden1_low, 'tensor', axis=0, tiled=True)  112 us
    all_gather x1, waiting for transfers between devices, local(): group_rows = lax.all_gather(tokens, 'tensor', axis=0, tiled=True)  93.6 us
    all_gather x1, waiting for transfers between devices, local(): group_d_attn = lax.all_gather(d_attn_low, 'tensor', axis=0, tiled=True)  92.8 us
    dot_general x24, matrix products, make_scores(): jnp.einsum('qd,kd->qk', queries, key_rows, preferred_element_type=jnp.flo...  73 us
  transfers between devices with their start and end apart: 14, of which 11 were waited for; matrix products, arithmetic and copies ran while one was open for 16% of the time, Pallas kernels for 0%

commit v1 on v0

--- a/solution.py
+++ b/solution.py
@@ -9,6 +9,18 @@
 NORM_EPS = 1e-12
 INV_ROOT_TWO = 0.7071067811865476
 INV_ROOT_TWO_PI = 0.3989422804014327
+
+
+def collect(value, axis, dim):
+    ways, here = (lax.axis_size(axis), lax.axis_index(axis))
+    grown, reach = (value, 1)
+    while reach < ways:
+        theirs = lax.ppermute(grown, axis, [(d, d ^ reach) for d in range(ways)])
+        mine_first = jnp.concatenate([grown, theirs], axis=dim)
+        theirs_first = jnp.concatenate([theirs, grown], axis=dim)
+        grown = jnp.where(here & reach == 0, mine_first, theirs_first)
+        reach = 2 * reach
+    return grown
 
 
 def head_slopes(first_head, head_count):
@@ -149,7 +161,7 @@
     resid1 = tokens.astype(jnp.float32) + attention + out_bias
     hidden1, normed1, inverse1 = norm_forward(resid1, norm1_gain, norm1_shift)
     hidden1_low = hidden1.astype(jnp.bfloat16)
-    group_hidden = lax.all_gather(hidden1_low, "tensor", axis=0, tiled=True)
+    group_hidden = collect(hidden1_low, "tensor", 0)
     gate_up = jnp.dot(
         group_hidden,
         in_full.reshape(model_width, 2 * hidden_width),

time: 1850 us -> 1920 us (1.038)
  waiting for transfers between devices: 1190 us -> 1240 us
    ppermute x0 -> x2, waiting for transfers between devices: none -> 166 us  [collect(): theirs = lax.ppermute(grown, axis, [(d, d ^ reach) for d in range(ways)])]
    all_gather x1 -> x0, waiting for transfers between devices: 112 us -> none  [local(): group_hidden = lax.all_gather(hidden1_low, 'tensor', axis=0, tiled=True)]
  transfers between devices with their start and end apart: 14 -> 15, of which waited for: 11 -> 12; matrix products, arithmetic and copies ran while one was open for 16% -> 16% of each run, Pallas kernels for 0% -> 0%
where the time goes in v1:
time: 1920 us; the launch traced here: 1910 us
  waiting for transfers between devices  1240 us (65%)
  matrix products  352 us (18%)
  local copies, waits for them, and re-layouts  134 us (7%)
  other arithmetic  72.4 us (4%)
  blocking collectives  70.7 us (4%)
    reduce_scatter x1, waiting for transfers between devices, local(): lax.psum_scatter(d_group_hidden, 'tensor', scatter_dimension=0, tiled=True)  210 us
    reduce_scatter x1, waiting for transfers between devices, local(): lax.psum_scatter(attn_partial, 'tensor', scatter_dimension=0, tiled=True)  210 us
    reduce_scatter x1, waiting for transfers between devices, local(): lax.psum_scatter(ffn_partial, 'tensor', scatter_dimension=0, tiled=True)  202 us
    ppermute x2, waiting for transfers between devices, collect(): theirs = lax.ppermute(grown, axis, [(d, d ^ reach) for d in range(ways)])  166 us
    all_gather x1, waiting for transfers between devices, local(): group_d_ffn = lax.all_gather(d_ffn_low, 'tensor', axis=0, tiled=True)  117 us
    all_gather x1, waiting for transfers between devices, local(): group_rows = lax.all_gather(tokens, 'tensor', axis=0, tiled=True)  93.6 us
    all_gather x1, waiting for transfers between devices, local(): group_d_attn = lax.all_gather(d_attn_low, 'tensor', axis=0, tiled=True)  88.9 us
    dot_general x24, matrix products, make_scores(): jnp.einsum('qd,kd->qk', queries, key_rows, preferred_element_type=jnp.flo...  73 us
  transfers between devices with their start and end apart: 15, of which 12 were waited for; matrix products, arithmetic and copies ran while one was open for 16% of the time, Pallas kernels for 0%

profile of v1, /device:TPU:0, one launch (start us, length us, event | category | flops | bytes accessed | tf_op | source)
XLA Modules:
  0.0 1906.8 jit_solution(17056025330861012192)
XLA Ops:
  10.0 14.6 all_gather.26
  34.9 93.6 %all-gather.6.cloned.1.call-done = bf16[4096,768]{1,0:T(8,128)(2,1)} async-done(((bf16[1024,768]{1,0:T(8,128)(2,1)}), bf16[4096,768]{1,0:T(8,128)(2,1)}) %all-gather.6.cloned.1.call-update) | async-done | bytes 6291472 | tf_op jit(solution)/shard_map/all_gather | solution.py:140
  160.0 131.6 %while.26 = (s32[]{:T(128)}, bf16[12,1024,64]{1,2,0:T(8,128)(2,1)}, f32[12,1024]{1,0:T(8,128)}, bf16[12,1024,64]{2,1,0:T(8,128)(2,1)S(1)}, bf16[12,1024,64]{2,1,...) while((s32[]{:T(128)}, bf16[12,1024,64]{1,2,0:T(8,128)(2,1)}, ...), condition=%wide.region_3.4_spmd, body=%wide.region_0.3_spmd.sunk | while | flops 280034304 | bytes 30321288 | solution.py:155
  303.9 209.9 %reduce-scatter.8.cloned.1.call-done = f32[1024,768]{1,0:T(8,128)} async-done(((f32[4096,768]{1,0:T(8,128)}), f32[1024,768]{1,0:T(8,128)}) %reduce-scatter.8.cloned.1.call-update) | async-done | bytes 3145744 | tf_op jit(solution)/shard_map/reduce_scatter | solution.py:160
  520.6 34.9 %collective-permute-done = bf16[1024,768]{1,0:T(8,128)(2,1)} collective-permute-done((bf16[1024,768]{1,0:T(8,128)(2,1)}, bf16[1024,768]{1,0:T(8,128)(2,1)}, u32[]{:S(2)}, u32[]{:S(2)}) %collective-permute-start) | collective-permute-done | bytes 1572896 | tf_op jit(solution)/shard_map/ppermute | solution.py:18
  567.3 131.2 %collective-permute-done.1 = bf16[2048,768]{1,0:T(8,128)(2,1)} collective-permute-done((bf16[2048,768]{1,0:T(8,128)(2,1)}, bf16[2048,768]{1,0:T(8,128)(2,1)}, u32[]{:S(2)}, u32[]{:S(2)}) %collective-permute-start.1) | collective-permute-done | bytes 3145760 | tf_op jit(solution)/shard_map/ppermute | solution.py:18
  698.5 20.0 %fusion.63 = f32[4096,1536]{0,1:T(8,128)} fusion(bf16[768,1536]{1,0:T(8,128)(2,1)} %bitcast.195, bf16[2048,768]{1,0:T(8,128)(2,1)} %collective-permute-done.1, bf16[2048,768]{1,0:T(8,128)(2,1)} %maximum_select_fusion.1, pred[]{:T(512)S(6)} %eq.6), kind=kOutput, calls=%fused_computation.102 | convolution fusion | flops 9691987968 | bytes 33816576 | tf_op jit(solution)/shard_map/dot_general | solution.py:165
  718.5 12.1 multiply_convert_fusion.2
  730.7 10.3 fusion.78
  741.0 10.0 all-gather.12.cloned.1.call-start
  751.1 202.1 %reduce-scatter.10.cloned.1.call-done = f32[1024,768]{1,0:T(8,128)} async-done(((f32[4096,768]{1,0:T(8,128)}), f32[1024,768]{1,0:T(8,128)}) %reduce-scatter.10.cloned.1.call-update) | async-done | bytes 3145744 | tf_op jit(solution)/shard_map/reduce_scatter | solution.py:175
  965.8 116.5 %all-gather.12.cloned.1.call-done = bf16[4096,768]{1,0:T(8,128)(2,1)} async-done(((bf16[1024,768]{1,0:T(8,128)(2,1)}), bf16[4096,768]{1,0:T(8,128)(2,1)}) %all-gather.12.cloned.1.call-update) | async-done | bytes 6291472 | tf_op jit(solution)/shard_map/all_gather | solution.py:183
  1082.3 22.1 %fusion.50 = (bf16[4096,768]{0,1:T(8,128)(2,1)}, bf16[4096,768]{0,1:T(8,128)(2,1)}) fusion(f32[4096,1536]{0,1:T(8,128)} %fusion.63, bf16[4096,768]{1,0:T(8,128)(2,1)} %all-gather.12.cloned.1.call-done, bf16[768,768]{1,0:T(8,128)(2,1)} %all-gather.10.cloned.1.call-done), kind=kOutput, calls=%fused_computation.57 | convolution fusion | flops 4875878400 | bytes 45219840 | tf_op jit(solution)/shard_map/dot_general | solution.py:187
  1104.3 16.1 fusion.52
  1120.5 210.2 %reduce-scatter.12.cloned.1.call-done = f32[1024,768]{1,0:T(8,128)} async-done(((f32[4096,768]{1,0:T(8,128)}), f32[1024,768]{1,0:T(8,128)}) %reduce-scatter.12.cloned.1.call-update) | async-done | bytes 3145744 | tf_op jit(solution)/shard_map/reduce_scatter | solution.py:201
  1339.2 20.4 %fusion.51 = f32[768,1536]{1,0:T(8,128)} fusion(bf16[4096,768]{0,1:T(8,128)(2,1)} %get-tuple-element.173, bf16[4096,768]{0,1:T(8,128)(2,1)} %get-tuple-element.172, bf16[2048,768]{1,0:T(8,128)(2,1)} %collective-permute-done.1, bf16[2048,768]{1,0:T(8,128)(2,1)} %maximum_select_fusion.1, pred[]{:T(512)S(6)} %eq.6), kind=kOutput, calls=%fused_computation.63 | convolution fusion | flops 9717153792 | bytes 23592960 | tf_op jit(solution)/shard_map/rd,rc->dc/dot_general | solution.py:192
  1366.4 88.9 %all-gather.14.cloned.1.call-done = bf16[4096,768]{1,0:T(8,128)(2,1)} async-done(((bf16[1024,768]{1,0:T(8,128)(2,1)}), bf16[4096,768]{1,0:T(8,128)(2,1)}) %all-gather.14.cloned.1.call-update) | async-done | bytes 6291472 | tf_op jit(solution)/shard_map/all_gather | solution.py:208
  1469.8 167.6 %while.27 = (s32[]{:T(128)}, f32[12,1024,64]{1,2,0:T(8,128)S(1)}, bf16[12,1024,64]{1,2,0:T(8,128)(2,1)}, f32[12,1024,64]{1,2,0:T(8,128)}, bf16[12,1024,64]{2,1,0...) while((s32[]{:T(128)}, f32[12,1024,64]{1,2,0:T(8,128)S(1)}, ...), condition=%wide.region_17.18_spmd, body=%wide.region_15.17_spmd.sunk | while | flops 683801600 | bytes 34104956 | solution.py:213
  1656.1 10.4 fusion.81
  1693.8 47.5 %all-reduce.1 = (f32[2,768]{1,0:T(2,128)}, f32[768]{0:T(1024)}, f32[768]{0:T(1024)}, f32[768]{0:T(1024)}, f32[768]{0:T(1024)}, /*index=5*/f32[768]{0:T(1024)}, f32[768]{0:T(1024)}) all-reduce(f32[2,768]{1,0:T(2,128)S(1)} %dynamic_update_slice.21, ...), channel_id=1, replica_groups=mesh['dp'=8,'tensor'=4] {'dp','tensor'}, use_global_device_ids=true, to_apply=%region_22.23 | all-reduce | flops 6144 | bytes 49152 | tf_op jit(solution)/shard_map/psum | solution.py:261
  1741.3 24.9 %reduce-scatter.14.cloned.1.call-done = bf16[1024,768]{1,0:T(8,128)(2,1)} async-done(((bf16[4096,768]{1,0:T(8,128)(2,1)}), bf16[1024,768]{1,0:T(8,128)(2,1)}) %reduce-scatter.14.cloned.1.call-update) | async-done | bytes 1572880 | tf_op jit(solution)/shard_map/reduce_scatter | solution.py:243
  1769.1 44.1 %reduce-scatter.20.cloned.1.call-done = f32[96,768]{1,0:T(8,128)} async-done(((f32[768,768]{1,0:T(8,128)}), f32[96,768]{1,0:T(8,128)}) %reduce-scatter.20.cloned.1.call-update) | async-done | bytes 294928 | tf_op jit(solution)/shard_map/reduce_scatter | solution.py:251
  1813.1 39.1 %reduce-scatter.18.cloned.1.call-done = f32[96,192]{1,0:T(8,128)} async-done(((f32[768,192]{1,0:T(8,128)}), f32[96,192]{1,0:T(8,128)}) %reduce-scatter.18.cloned.1.call-update) | async-done | bytes 73744 | tf_op jit(solution)/shard_map/reduce_scatter | solution.py:250
  1852.2 46.6 %reduce-scatter.16.cloned.1.call-done = f32[96,3,192]{2,0,1:T(8,128)} async-done(((f32[768,3,192]{2,0,1:T(8,128)}), f32[96,3,192]{2,0,1:T(8,128)}) %reduce-scatter.16.cloned.1.call-update) | async-done | bytes 221200 | tf_op jit(solution)/shard_map/reduce_scatter | solution.py:248
  (349 shorter events, 463.0 us)
Async XLA Ops:
  8.0 17.5 copy-start.17
  8.0 120.5 %all-gather.6.cloned.1.call-start = ((), (), s32[]{:S(2)}) async-start(), calls=%async_computation.7 | async-start | bytes 7864320 | tf_op jit(solution)/shard_map/all_gather | solution.py:140
  8.8 505.1 %reduce-scatter.8.cloned.1.call-start = ((), (), s32[]{:S(2)}) async-start(), calls=%async_computation.8 | async-start | bytes 15728640 | tf_op jit(solution)/shard_map/reduce_scatter | solution.py:160
  25.5 109.0 %copy-start.13 = (bf16[768,3,192]{0,2,1:T(8,128)(2,1)}, bf16[768,3,192]{0,2,1:T(8,128)(2,1)S(1)}, u32[]{:S(2)}) copy-start(bf16[768,3,192]{0,2,1:T(8,128)(2,1)S(1)} %copy.42) | copy-start | bytes 2654212
  34.1 261.9 %copy-start.9 = (bf16[768,192]{1,0:T(8,128)(2,1)}, bf16[768,192]{1,0:T(8,128)(2,1)S(1)}, u32[]{:S(2)}) copy-start(bf16[768,192]{1,0:T(8,128)(2,1)S(1)} %all_gather.27) | copy-start | bytes 884740
  303.6 210.3 %copy-start.24 = (f32[768]{0:T(1024)S(1)}, f32[768]{0:T(1024)}, u32[]{:S(2)}) copy-start(f32[768]{0:T(1024)} %param.21) | copy-start | bytes 9220
  303.6 260.0 %all-gather.8.cloned.1.call-start = ((), (), s32[]{:S(2)}) async-start(), calls=%async_computation.9 | async-start | bytes 2654208 | tf_op jit(solution)/shard_map/all_gather | solution.py:104
  519.1 36.5 %collective-permute-start = (bf16[1024,768]{1,0:T(8,128)(2,1)}, bf16[1024,768]{1,0:T(8,128)(2,1)}, u32[]{:S(2)}, u32[]{:S(2)}) collective-permute-start(bf16[1024,768]{1,0:T(8,128)(2,1)} %fusion.62), channel_id=1, source_target_pairs={{0,1},{1,0},{2,3},{3,2},{4,5},{5,4},{6,7},{7,6},{8,9},{9,8},{10,11... | collective-permute-start | bytes 4718600 | tf_op jit(solution)/shard_map/ppermute | solution.py:18
  520.6 210.1 %all-gather.10.cloned.1.call-start = ((), (), s32[]{:S(2)}) async-start(), calls=%async_computation.10 | async-start | bytes 1327104 | tf_op jit(solution)/shard_map/all_gather | solution.py:106
  560.0 138.5 %collective-permute-start.1 = (bf16[2048,768]{1,0:T(8,128)(2,1)}, bf16[2048,768]{1,0:T(8,128)(2,1)}, u32[]{:S(2)}, u32[]{:S(2)}) collective-permute-start(bf16[2048,768]{1,0:T(8,128)(2,1)} %maximum_select_fusion.1), channel_id=1, source_target_pairs={{0,2},{1,3},{2,0},{3,1},{4,6},{5,7},{6,4},{7,5},{8,10},{9,11},{10,... | collective-permute-start | bytes 9437192 | tf_op jit(solution)/shard_map/ppermute | solution.py:18
  563.5 389.7 %reduce-scatter.10.cloned.1.call-start = ((), (), s32[]{:S(2)}) async-start(), calls=%async_computation.11 | async-start | bytes 15728640 | tf_op jit(solution)/shard_map/reduce_scatter | solution.py:175
  741.0 212.2 %copy-start.25 = (f32[768]{0:T(1024)S(1)}, f32[768]{0:T(1024)}, u32[]{:S(2)}) copy-start(f32[768]{0:T(1024)} %param.26) | copy-start | bytes 9220
  741.0 341.2 %all-gather.12.cloned.1.call-start = ((), (), s32[]{:S(2)}) async-start(), calls=%async_computation.12 | async-start | bytes 7864320 | tf_op jit(solution)/shard_map/all_gather | solution.py:183
  965.7 365.0 %reduce-scatter.12.cloned.1.call-start = ((), (), s32[]{:S(2)}) async-start(), calls=%async_computation.13 | async-start | bytes 15728640 | tf_op jit(solution)/shard_map/reduce_scatter | solution.py:201
  1082.3 22.1 %copy-start.11 = (bf16[96,8,2,768]{3,1,2,0:T(8,128)(2,1)S(1)}, bf16[96,8,2,768]{3,1,2,0:T(8,128)(2,1)}, u32[]{:S(2)}) copy-start(bf16[96,8,2,768]{3,1,2,0:T(8,128)(2,1)} %copy.53) | copy-start | bytes 7077892
  1120.5 334.8 %all-gather.14.cloned.1.call-start = ((), (), s32[]{:S(2)}) async-start(), calls=%async_computation.14 | async-start | bytes 7864320 | tf_op jit(solution)/shard_map/all_gather | solution.py:208
  1338.7 344.3 %all-reduce.4.cloned.1.call-start = ((), (), s32[]{:S(2)}) async-start(), calls=%async_computation.19 | async-start | bytes 9437184
  1366.3 89.0 %copy-start.10 = (bf16[768,192]{1,0:T(8,128)(2,1)S(1)}, bf16[768,192]{1,0:T(8,128)(2,1)}, u32[]{:S(2)}) copy-start(bf16[768,192]{1,0:T(8,128)(2,1)} %copy-done.9) | copy-start | bytes 884740
  1366.4 399.8 %reduce-scatter.14.cloned.1.call-start = ((), (), s32[]{:S(2)}) async-start(), calls=%async_computation.15 | async-start | bytes 7864320 | tf_op jit(solution)/shard_map/reduce_scatter | solution.py:243
  1656.0 10.6 copy-start.6
  1656.0 157.1 %reduce-scatter.20.cloned.1.call-start = ((), (), s32[]{:S(2)}) async-start(), calls=%async_computation.18 | async-start | bytes 2654208 | tf_op jit(solution)/shard_map/reduce_scatter | solution.py:251
  1666.6 185.6 %reduce-scatter.18.cloned.1.call-start = ((), (), s32[]{:S(2)}) async-start(), calls=%async_computation.17 | async-start | bytes 884736 | tf_op jit(solution)/shard_map/reduce_scatter | solution.py:250
  1672.2 226.6 %reduce-scatter.16.cloned.1.call-start = ((), (), s32[]{:S(2)}) async-start(), calls=%async_computation.16 | async-start | bytes 2654208 | tf_op jit(solution)/shard_map/reduce_scatter | solution.py:248
  1685.0 81.2 %copy-start.3 = (f32[1024,768]{1,0:T(8,128)S(1)}, f32[1024,768]{1,0:T(8,128)}, u32[]{:S(2)}) copy-start(f32[1024,768]{1,0:T(8,128)} %copy-done.2) | copy-start | bytes 9437188
  (31 other events, 86.6 us)
Sparse Core Ops, SparseCore 0:
  10.4 118.0 all-gather.5
  303.7 210.0 reduce-scatter.7
  741.2 211.9 reduce-scatter.9
  965.8 116.3 all-gather.11
  1120.6 210.0 reduce-scatter.11
  1338.9 116.4 all-gather.13
  1656.2 109.9 reduce-scatter.13
  1770.1 42.9 reduce-scatter.19
  1817.2 34.9 reduce-scatter.17
  1856.3 42.4 reduce-scatter.15
Sparse Core Ops, SparseCore 1:
  520.7 29.8 all-gather.7
  563.6 22.0 all-gather.9
  1366.4 87.4 all-reduce.3
